TPU v7x, 32 devices: a whole 2x2x4 slice. The times are simulated.
32 devices in a mesh: ctx: 8 (over y, x, core), fsdp: 4 (over z).
Axes of the slice: x: 2, y: 2, z: 4, core: 2. Of those that a mesh axis runs over, the one named last changes fastest.
Arguments:
- layer_in: bfloat16 [4, 1024, 1600], P('fsdp', 'ctx'), may hold values from -6 to 6
- out_cot: bfloat16 [4, 1024, 1600], P('fsdp', 'ctx'), may hold values from -6 to 6
- first_gain: bfloat16 [1600], P('fsdp'), may hold values from 0.5 to 1.5
- first_bias: bfloat16 [1600], P('fsdp'), may hold values from -3 to 3
- qkv_weight: bfloat16 [1600, 4800], P('fsdp'), may hold values from -0.15625 to 0.15625
- qv_bias: bfloat16 [2, 1600], P(None, 'fsdp'), may hold values from -3 to 3
- out_weight: bfloat16 [1600, 1600], P('fsdp'), may hold values from -0.625 to 0.625
- out_bias: bfloat16 [1600], P('fsdp'), may hold values from -3 to 3
- second_gain: bfloat16 [1600], P('fsdp'), may hold values from 0.5 to 1.5
- second_bias: bfloat16 [1600], P('fsdp'), may hold values from -3 to 3
- fc_weight: bfloat16 [1600, 6400], P('fsdp'), may hold values from -0.15625 to 0.15625
- fc_bias: bfloat16 [6400], P('fsdp'), may hold values from -3 to 3
- proj_weight: bfloat16 [6400, 1600], P(None, 'fsdp'), may hold values from -0.078125 to 0.078125
- proj_bias: bfloat16 [1600], P('fsdp'), may hold values from -3 to 3
Outputs:
- layer_out: bfloat16 [4, 1024, 1600], P('fsdp', 'ctx')
- grad_in: bfloat16 [4, 1024, 1600], P('fsdp', 'ctx')
- grad_first_gain: float32 [1600], P('fsdp')
- grad_first_bias: float32 [1600], P('fsdp')
- grad_qkv_weight: float32 [1600, 4800], P('fsdp')
- grad_qv_bias: float32 [2, 1600], P(None, 'fsdp')
- grad_out_weight: float32 [1600, 1600], P('fsdp')
- grad_out_bias: float32 [1600], P('fsdp')
- grad_second_gain: float32 [1600], P('fsdp')
- grad_second_bias: float32 [1600], P('fsdp')
- grad_fc_weight: float32 [1600, 6400], P('fsdp')
- grad_fc_bias: float32 [6400], P('fsdp')
- grad_proj_weight: float32 [6400, 1600], P(None, 'fsdp')
- grad_proj_bias: float32 [1600], P('fsdp')
All inputs are finite; a program needn't handle non-finite values.
Results may differ from a plain program's by a relative error of at most 0.03.
Values may be sent and summed in bfloat16 or wider, within the bound.
No kernel may reach another device: no remote copies, remote signals or barrier semaphores. Data moves between devices by JAX's collectives and lax.ppermute only.
A program may use at most 512 MiB of HBM per device.

v0:
```python
import math
import jax
import jax.numpy as jnp
from jax import lax
from jax.sharding import PartitionSpec as P

D = 1600
H = 25
HD = 64


def norm_apply(values, norm_gain, norm_bias):
    centre = jnp.mean(values, axis=-1, keepdims=True)
    shifted = values - centre
    spread = jnp.mean(shifted * shifted, axis=-1, keepdims=True)
    return shifted * lax.rsqrt(spread + 1e-05) * norm_gain + norm_bias


def contract_rows(left, right):
    return lax.dot_general(
        left, right, (((0,), (0,)), ((), ())), preferred_element_type=jnp.float32
    )


def contract_cols(left, right):
    return lax.dot_general(
        left, right, (((1,), (1,)), ((), ())), preferred_element_type=jnp.float32
    )


def split_product(form, weights, other):
    upper = weights.astype(jnp.bfloat16)
    lower = (weights - upper.astype(jnp.float32)).astype(jnp.bfloat16)
    return jnp.einsum(form, upper, other, preferred_element_type=jnp.float32) + jnp.einsum(
        form, lower, other, preferred_element_type=jnp.float32
    )


def sweep_blocks(running, piece_rows, handle):
    block_rows = 512
    return lax.fori_loop(
        0,
        piece_rows // block_rows,
        lambda block_index, state_now: handle(state_now, block_index * block_rows, block_rows),
        running,
    )


def on_device(
    layer_in,
    out_cot,
    first_gain,
    first_bias,
    qkv_weight,
    qv_bias,
    out_weight,
    out_bias,
    second_gain,
    second_bias,
    fc_weight,
    fc_bias,
    proj_weight,
    proj_bias,
):
    f32 = jnp.float32
    bf16 = jnp.bfloat16
    factor = 1.0 / math.sqrt(HD)
    gathered = (
        lax.all_gather(first_gain, "fsdp", axis=0, tiled=True),
        lax.all_gather(first_bias, "fsdp", axis=0, tiled=True),
        lax.all_gather(qkv_weight, "fsdp", axis=0, tiled=True),
        lax.all_gather(qv_bias, "fsdp", axis=1, tiled=True),
        lax.all_gather(out_weight, "fsdp", axis=0, tiled=True),
        lax.all_gather(out_bias, "fsdp", axis=0, tiled=True),
        lax.all_gather(second_gain, "fsdp", axis=0, tiled=True),
        lax.all_gather(second_bias, "fsdp", axis=0, tiled=True),
        lax.all_gather(fc_weight, "fsdp", axis=0, tiled=True),
        lax.all_gather(fc_bias, "fsdp", axis=0, tiled=True),
        lax.all_gather(proj_weight, "fsdp", axis=1, tiled=True),
        lax.all_gather(proj_bias, "fsdp", axis=0, tiled=True),
    )
    gain_one = gathered[0].astype(f32)
    bias_one = gathered[1].astype(f32)
    full_qkv = gathered[2]
    bias_qv = gathered[3].astype(f32)
    full_out = gathered[4]
    bias_out = gathered[5].astype(f32)
    gain_two = gathered[6].astype(f32)
    bias_two = gathered[7].astype(f32)
    full_fc = gathered[8]
    bias_fc = gathered[9].astype(f32)
    full_proj = gathered[10]
    bias_proj = gathered[11].astype(f32)
    tokens = layer_in[0].astype(f32)
    local_rows = tokens.shape[0]
    offset = lax.axis_index("ctx") * local_rows
    query_pos = offset + jnp.arange(local_rows, dtype=jnp.int32)
    normed_one = norm_apply(tokens, gain_one, bias_one).astype(bf16)
    projected = jnp.dot(normed_one, full_qkv, preferred_element_type=f32)
    queries = (projected[:, 0:D] + bias_qv[0]).astype(bf16)
    key_rows = projected[:, D : 2 * D].astype(bf16)
    value_rows = (projected[:, 2 * D : 3 * D] + bias_qv[1]).astype(bf16)
    query_heads = queries.reshape(local_rows, H, HD)
    start_state = (
        jnp.full((H, local_rows), -1e30, f32),
        jnp.zeros((H, local_rows), f32),
        jnp.zeros((local_rows, H, HD), f32),
    )
    key_piece = lax.all_gather(key_rows, "ctx", axis=0, tiled=True)
    value_piece = lax.all_gather(value_rows, "ctx", axis=0, tiled=True)

    def forward_step(state_now, begin_row, block_rows):
        row_max, row_total, accum = state_now
        key_block = lax.dynamic_slice_in_dim(key_piece, begin_row, block_rows, 0).reshape(
            block_rows, H, HD
        )
        value_block = lax.dynamic_slice_in_dim(value_piece, begin_row, block_rows, 0).reshape(
            block_rows, H, HD
        )
        key_pos = begin_row + jnp.arange(block_rows, dtype=jnp.int32)
        allowed = (key_pos[None, :] <= query_pos[:, None])[None]
        scores = (
            jnp.einsum("qhd,khd->hqk", query_heads, key_block, preferred_element_type=f32) * factor
        )
        masked = jnp.where(allowed, scores, -1e30)
        new_max = jnp.maximum(row_max, jnp.max(masked, axis=-1))
        weights = jnp.where(allowed, jnp.exp(masked - new_max[:, :, None]), 0.0)
        rescale = jnp.exp(row_max - new_max)
        new_total = row_total * rescale + jnp.sum(weights, axis=-1)
        update = split_product("hqk,khd->qhd", weights, value_block)
        new_accum = accum * rescale.T[:, :, None] + update
        return (new_max, new_total, new_accum)

    row_max, row_total, accum = sweep_blocks(start_state, key_piece.shape[0], forward_step)
    attn_heads = accum / row_total.T[:, :, None]
    log_total = row_max + jnp.log(row_total)
    attn_out = attn_heads.reshape(local_rows, D).astype(bf16)
    resid = tokens + jnp.dot(attn_out, full_out, preferred_element_type=f32) + bias_out
    normed_two = norm_apply(resid, gain_two, bias_two).astype(bf16)
    pre_act = jnp.dot(normed_two, full_fc, preferred_element_type=f32) + bias_fc
    activated = jax.nn.gelu(pre_act, approximate=True).astype(bf16)
    mlp_out = jnp.dot(activated, full_proj, preferred_element_type=f32) + bias_proj
    layer_out = (resid + mlp_out).astype(bf16)[None]
    cotangent = out_cot[0]
    cot_float = cotangent.astype(f32)
    grad_proj = contract_rows(activated, cotangent)
    grad_proj_b = jnp.sum(cot_float, axis=0)
    d_activated = contract_cols(cotangent, full_proj)
    unused_value, gelu_back = jax.vjp(lambda inner: jax.nn.gelu(inner, approximate=True), pre_act)
    d_pre = gelu_back(d_activated)[0].astype(bf16)
    grad_fc = contract_rows(normed_two, d_pre)
    grad_fc_b = jnp.sum(d_pre.astype(f32), axis=0)
    d_norm_two = contract_cols(d_pre, full_fc)
    unused_two, norm_back_two = jax.vjp(norm_apply, resid, gain_two, bias_two)
    d_resid_norm, grad_gain_two, grad_bias_two = norm_back_two(d_norm_two)
    d_resid = cot_float + d_resid_norm
    d_branch = d_resid.astype(bf16)
    mlp_parts = (
        lax.psum_scatter(
            grad_gain_two.astype(jnp.bfloat16), "fsdp", scatter_dimension=0, tiled=True
        ).astype(jnp.float32),
        lax.psum_scatter(
            grad_bias_two.astype(jnp.bfloat16), "fsdp", scatter_dimension=0, tiled=True
        ).astype(jnp.float32),
        lax.psum_scatter(
            grad_fc.astype(jnp.bfloat16), "fsdp", scatter_dimension=0, tiled=True
        ).astype(jnp.float32),
        lax.psum_scatter(
            grad_fc_b.astype(jnp.bfloat16), "fsdp", scatter_dimension=0, tiled=True
        ).astype(jnp.float32),
        lax.psum_scatter(
            grad_proj.astype(jnp.bfloat16), "fsdp", scatter_dimension=1, tiled=True
        ).astype(jnp.float32),
        lax.psum_scatter(
            grad_proj_b.astype(jnp.bfloat16), "fsdp", scatter_dimension=0, tiled=True
        ).astype(jnp.float32),
    )
    mlp_parts = (
        lax.psum(mlp_parts[0].astype(jnp.bfloat16), "ctx").astype(jnp.float32),
        lax.psum(mlp_parts[1].astype(jnp.bfloat16), "ctx").astype(jnp.float32),
        lax.psum(mlp_parts[2].astype(jnp.bfloat16), "ctx").astype(jnp.float32),
        lax.psum(mlp_parts[3].astype(jnp.bfloat16), "ctx").astype(jnp.float32),
        lax.psum(mlp_parts[4].astype(jnp.bfloat16), "ctx").astype(jnp.float32),
        lax.psum(mlp_parts[5].astype(jnp.bfloat16), "ctx").astype(jnp.float32),
    )
    grad_out = contract_rows(attn_out, d_branch)
    grad_out_b = jnp.sum(d_branch.astype(f32), axis=0)
    d_attn = contract_cols(d_branch, full_out).astype(bf16)
    d_attn_heads = d_attn.reshape(local_rows, H, HD)
    delta_cols = jnp.sum(d_attn_heads.astype(f32) * attn_heads, axis=-1)
    delta_rows = delta_cols.T
    seq_rows = lax.axis_size("ctx") * local_rows

    def block_weights(query_block, key_block, lse_block, query_at, key_at):
        allowed = (key_at[None, :] <= query_at[:, None])[None]
        scores = (
            jnp.einsum("qhd,khd->hqk", query_block, key_block, preferred_element_type=f32) * factor
        )
        return jnp.where(allowed, jnp.exp(scores - lse_block[:, :, None]), 0.0)

    buffer_start = jnp.zeros((seq_rows, 2 * D), f32)
    back_start = (jnp.zeros((local_rows, H, HD), f32), buffer_start)
    query_key_piece = lax.all_gather(key_rows, "ctx", axis=0, tiled=True)
    query_value_piece = lax.all_gather(value_rows, "ctx", axis=0, tiled=True)

    def backward_step(state_now, begin_row, block_rows):
        d_query_sum, kv_buffer = state_now
        key_block = lax.dynamic_slice_in_dim(query_key_piece, begin_row, block_rows, 0).reshape(
            block_rows, H, HD
        )
        value_block = lax.dynamic_slice_in_dim(query_value_piece, begin_row, block_rows, 0).reshape(
            block_rows, H, HD
        )
        key_pos = begin_row + jnp.arange(block_rows, dtype=jnp.int32)
        weights = block_weights(query_heads, key_block, log_total, query_pos, key_pos)
        d_weights = jnp.einsum(
            "qhd,khd->hqk", d_attn_heads, value_block, preferred_element_type=f32
        )
        d_scores = (weights * (d_weights - delta_rows[:, :, None])).astype(bf16)
        d_query_sum = (
            d_query_sum
            + jnp.einsum("hqk,khd->qhd", d_scores, key_block, preferred_element_type=f32) * factor
        )
        d_key_block = (
            jnp.einsum("hqk,qhd->khd", d_scores, query_heads, preferred_element_type=f32) * factor
        )
        d_value_block = split_product("hqk,qhd->khd", weights, d_attn_heads)
        zero_col = jnp.zeros((), jnp.int32)
        current = lax.dynamic_slice(kv_buffer, (begin_row, zero_col), (block_rows, 2 * D))
        added = current + jnp.concatenate(
            [d_key_block.reshape(block_rows, D), d_value_block.reshape(block_rows, D)], axis=1
        )
        kv_buffer = lax.dynamic_update_slice(kv_buffer, added, (begin_row, zero_col))
        return (d_query_sum, kv_buffer)

    d_query_sum, kv_buffer = sweep_blocks(back_start, query_key_piece.shape[0], backward_step)
    kv_mine = lax.psum_scatter(
        kv_buffer.astype(jnp.bfloat16), "ctx", scatter_dimension=0, tiled=True
    ).astype(jnp.float32)
    d_kv = kv_mine.astype(bf16)
    d_queries = d_query_sum.reshape(local_rows, D).astype(bf16)
    d_stack = jnp.concatenate([d_queries, d_kv], axis=1)
    grad_qkv = contract_rows(normed_one, d_stack)
    grad_qv_b = jnp.stack(
        [jnp.sum(d_queries.astype(f32), axis=0), jnp.sum(d_kv[:, D : 2 * D].astype(f32), axis=0)]
    )
    d_norm_one = contract_cols(d_stack, full_qkv)
    unused_one, norm_back_one = jax.vjp(norm_apply, tokens, gain_one, bias_one)
    d_in_norm, grad_gain_one, grad_bias_one = norm_back_one(d_norm_one)
    grad_in = (d_resid + d_in_norm).astype(bf16)[None]
    attn_parts = (
        lax.psum_scatter(
            grad_gain_one.astype(jnp.bfloat16), "fsdp", scatter_dimension=0, tiled=True
        ).astype(jnp.float32),
        lax.psum_scatter(
            grad_bias_one.astype(jnp.bfloat16), "fsdp", scatter_dimension=0, tiled=True
        ).astype(jnp.float32),
        lax.psum_scatter(
            grad_qkv.astype(jnp.bfloat16), "fsdp", scatter_dimension=0, tiled=True
        ).astype(jnp.float32),
        lax.psum_scatter(
            grad_qv_b.astype(jnp.bfloat16), "fsdp", scatter_dimension=1, tiled=True
        ).astype(jnp.float32),
        lax.psum_scatter(
            grad_out.astype(jnp.bfloat16), "fsdp", scatter_dimension=0, tiled=True
        ).astype(jnp.float32),
        lax.psum_scatter(
            grad_out_b.astype(jnp.bfloat16), "fsdp", scatter_dimension=0, tiled=True
        ).astype(jnp.float32),
    )
    attn_parts = (
        lax.psum(attn_parts[0].astype(jnp.bfloat16), "ctx").astype(jnp.float32),
        lax.psum(attn_parts[1].astype(jnp.bfloat16), "ctx").astype(jnp.float32),
        lax.psum(attn_parts[2].astype(jnp.bfloat16), "ctx").astype(jnp.float32),
        lax.psum(attn_parts[3].astype(jnp.bfloat16), "ctx").astype(jnp.float32),
        lax.psum(attn_parts[4].astype(jnp.bfloat16), "ctx").astype(jnp.float32),
        lax.psum(attn_parts[5].astype(jnp.bfloat16), "ctx").astype(jnp.float32),
    )
    summed = (
        attn_parts[0],
        attn_parts[1],
        attn_parts[2],
        attn_parts[3],
        attn_parts[4],
        attn_parts[5],
        mlp_parts[0],
        mlp_parts[1],
        mlp_parts[2],
        mlp_parts[3],
        mlp_parts[4],
        mlp_parts[5],
    )
    return (
        layer_out,
        grad_in,
        summed[0],
        summed[1],
        summed[2],
        summed[3],
        summed[4],
        summed[5],
        summed[6],
        summed[7],
        summed[8],
        summed[9],
        summed[10],
        summed[11],
    )


def solution(mesh):
    placed = (
        P("fsdp", "ctx", None),
        P("fsdp", "ctx", None),
        P("fsdp"),
        P("fsdp"),
        P("fsdp", None),
        P(None, "fsdp"),
        P("fsdp", None),
        P("fsdp"),
        P("fsdp"),
        P("fsdp"),
        P("fsdp", None),
        P("fsdp"),
        P(None, "fsdp"),
        P("fsdp"),
    )
    return jax.shard_map(
        on_device,
        mesh=mesh,
        in_specs=placed,
        out_specs=(
            P("fsdp", "ctx", None),
            P("fsdp", "ctx", None),
            P("fsdp"),
            P("fsdp"),
            P("fsdp", None),
            P(None, "fsdp"),
            P("fsdp", None),
            P("fsdp"),
            P("fsdp"),
            P("fsdp"),
            P("fsdp", None),
            P("fsdp"),
            P(None, "fsdp"),
            P("fsdp"),
        ),
        check_vma=False,
    )
```

profile of v0, /device:TPU:0, one launch (start us, length us, event | category | flops | bytes accessed | tf_op | source)
XLA Modules:
  0.0 2622.3 jit_solution(15926004353740264351)
XLA Ops:
  10.0 13.5 all-gather
  25.2 28.7 %all-reduce.17 = (bf16[1600]{0:T(1024)(128)(2,1)S(1)}, bf16[1600]{0:T(1024)(128)(2,1)S(1)}, bf16[1600]{0:T(1024)(128)(2,1)S(1)}, bf16[6400]{0:T(1024)(128)(2,1)S...) all-reduce(bf16[1600]{0:T(1024)(128)(2,1)S(1)} %dynamic-update-slic, ...), channel_id=1, replica_groups=mesh['ctx'=8,'fsdp'=4] {'fsdp'}, use_global_device_ids=true, to_apply=%add.1 | all-reduce | flops 14400 | bytes 57600
  54.5 226.2 %all-gather.8.cloned.1.call-done = bf16[1600,4800]{1,0:T(8,128)(2,1)} async-done(((bf16[400,4800]{1,0:T(8,128)(2,1)}), bf16[1600,4800]{1,0:T(8,128)(2,1)}) %all-gather.8.cloned.1.call-update) | async-done | bytes 15360016 | tf_op jit(solution)/shard_map/all_gather | solution.py:71
  280.8 12.3 fusion.80
  293.1 2.6 fusion.63
  295.8 1.9 slice.41
  300.1 27.5 %all-gather.12.cloned.1.call-done = bf16[1024,1600]{0,1:T(8,128)(2,1)} async-done(((bf16[128,1600]{0,1:T(8,128)(2,1)}), bf16[1024,1600]{0,1:T(8,128)(2,1)}) %all-gather.12.cloned.1.call-update) | async-done | bytes 3276816 | tf_op jit(solution)/shard_map/all_gather | solution.py:110
  327.6 35.9 %all-gather.10.cloned.1.call-done = bf16[1024,1600]{0,1:T(8,128)(2,1)} async-done(((bf16[128,1600]{0,1:T(8,128)(2,1)}), bf16[1024,1600]{0,1:T(8,128)(2,1)}) %all-gather.10.cloned.1.call-update) | async-done | bytes 3276816 | tf_op jit(solution)/shard_map/all_gather | solution.py:109
  363.5 20.4 while.34
  363.6 2.1 constant_dynamic-slice_fusion.6
  365.8 1.5 fusion.152
  367.3 1.6 fusion.154
  368.9 2.0 fusion.156
  370.9 2.5 fusion.157
  373.6 2.4 constant_dynamic-slice_fusion.6
  376.0 1.5 fusion.152
  377.5 1.6 fusion.154
  379.1 2.0 fusion.156
  381.1 2.5 fusion.157
  384.7 1.2 fusion.73
  386.0 78.4 %all-gather.14.cloned.1.call-done = bf16[1600,1600]{1,0:T(8,128)(2,1)} async-done(((bf16[400,1600]{1,0:T(8,128)(2,1)}), bf16[1600,1600]{1,0:T(8,128)(2,1)}) %all-gather.14.cloned.1.call-update) | async-done | bytes 5120016 | tf_op jit(solution)/shard_map/all_gather | solution.py:73
  464.3 4.8 fusion.88
  469.4 343.6 %all-gather.16.cloned.1.call-done = bf16[1600,6400]{1,0:T(8,128)(2,1)} async-done(((bf16[400,6400]{1,0:T(8,128)(2,1)}), bf16[1600,6400]{1,0:T(8,128)(2,1)}) %all-gather.16.cloned.1.call-update) | async-done | bytes 20480016 | tf_op jit(solution)/shard_map/all_gather | solution.py:77
  813.0 12.3 convolution_add_fusion
  825.3 336.6 %all-gather.18.cloned.1.call-done = bf16[6400,1600]{0,1:T(8,128)(2,1)} async-done(((bf16[6400,400]{0,1:T(8,128)(2,1)}), bf16[6400,1600]{0,1:T(8,128)(2,1)}) %all-gather.18.cloned.1.call-update) | async-done | bytes 20480016 | tf_op jit(solution)/shard_map/all_gather | solution.py:79
  1161.9 13.9 fusion.89
  1175.8 13.3 multiply_reduce_fusion
  1190.4 1.6 convolution_convert_fusion.4
  1192.2 6.3 broadcast_in_dim.138
  1198.5 38.6 %while.35 = (s32[]{:T(128)}, f32[128,25,64]{0,2,1:T(8,128)S(1)}, f32[1024,3200]{0,1:T(8,128)}, bf16[1024,1600]{0,1:T(8,128)(2,1)}, bf16[128,25,64]{0,2,1:T(8,128...) while((s32[]{:T(128)}, f32[128,25,64]{0,2,1:T(8,128)S(1)}, ...), condition=%wide.region_12.13_spmd.clone, body=%wide.region_11.12_spmd.clone.sunk | while | flops 1291739776 | bytes 84286680 | solution.py:41
  1198.7 2.1 constant_dynamic-slice_fusion.7
  1201.9 2.6 fusion.170
  1205.6 1.3 convolution_multiply_fusion.3
  1206.9 1.5 fusion.172
  1208.4 2.2 fusion.173
  1210.6 7.2 fusion.174
  1217.9 2.1 constant_dynamic-slice_fusion.7
  1221.2 2.6 fusion.170
  1224.9 1.3 convolution_multiply_fusion.3
  1226.2 1.5 fusion.172
  1227.6 2.2 fusion.173
  1229.8 7.2 fusion.174
  1237.1 8.6 convert_element_type.256
  1245.6 9.5 copy.61
  1256.2 3.9 convolution_convert_fusion.3
  1260.5 56.5 %reduce-scatter.19.cloned.1.call-done = bf16[128,3200]{1,0:T(8,128)(2,1)} async-done(((bf16[1024,3200]{1,0:T(8,128)(2,1)}), bf16[128,3200]{1,0:T(8,128)(2,1)}) %reduce-scatter.19.cloned.1.call-update) | async-done | bytes 819216
  1317.0 1.7 copy.62
  1318.8 8.5 convolution_convert_fusion.2
  1328.3 11.7 convolution_convert_fusion
  1341.7 10.4 convolution_convert_fusion.1
  1354.8 60.5 %reduce-scatter.13.cloned.1.call-done = bf16[400,1600]{1,0:T(8,128)(2,1)} async-done(((bf16[1600,1600]{1,0:T(8,128)(2,1)}), bf16[400,1600]{1,0:T(8,128)(2,1)}) %reduce-scatter.13.cloned.1.call-update) | async-done | bytes 1280016 | tf_op jit(solution)/shard_map/reduce_scatter | solution.py:264
  1415.3 263.4 %reduce-scatter.11.cloned.1.call-done = bf16[400,4800]{1,0:T(8,128)(2,1)} async-done(((bf16[1600,4800]{1,0:T(8,128)(2,1)}), bf16[400,4800]{1,0:T(8,128)(2,1)}) %reduce-scatter.11.cloned.1.call-update) | async-done | bytes 3840016 | tf_op jit(solution)/shard_map/reduce_scatter | solution.py:258
  1678.6 343.0 %reduce-scatter.17.cloned.1.call-done = bf16[6400,400]{0,1:T(8,128)(2,1)} async-done(((bf16[6400,1600]{0,1:T(8,128)(2,1)}), bf16[6400,400]{0,1:T(8,128)(2,1)}) %reduce-scatter.17.cloned.1.call-update) | async-done | bytes 5120016 | tf_op jit(solution)/shard_map/reduce_scatter | solution.py:171
  2021.6 343.3 %reduce-scatter.15.cloned.1.call-done = bf16[400,6400]{1,0:T(8,128)(2,1)} async-done(((bf16[1600,6400]{1,0:T(8,128)(2,1)}), bf16[400,6400]{1,0:T(8,128)(2,1)}) %reduce-scatter.15.cloned.1.call-update) | async-done | bytes 5120016 | tf_op jit(solution)/shard_map/reduce_scatter | solution.py:165
  2366.7 9.1 fusion.82
  2377.3 19.8 all-reduce.16
  2397.8 2.5 fusion.67
  2400.3 11.6 fusion.50
  2412.9 24.1 all-reduce.14
  2441.7 156.3 %all-reduce.20.cloned.1.call-done = (bf16[400,4800]{1,0:T(8,128)(2,1)}, bf16[400,1600]{1,0:T(8,128)(2,1)}, bf16[400,6400]{1,0:T(8,128)(2,1)}, bf16[6400,400]{0,1:T(8,128)(2,1)}) async-done(((bf16[400,4800]{1,0:T(8,128)(2,1)}, bf16[400,1600]{1,0:T(8,128)(2,1)}, bf16[400,6400]{1,0:T(8,128)(2,1)}, bf16[6400,400]{0,1:T(8,128)(2,1)}), (bf16[400,4800]{1,0:T(8,128)(2,1)}, bf16[400,1600]{1,0:T(8,128)(2,1)}, ...) | async-done | bytes 15360016 | tf_op jit(solution)/shard_map/psum | solution.py:274
  2598.1 3.1 convert_element_type.268
  2601.2 4.5 convert_element_type.263
  2606.2 4.7 convert_element_type.275
  2610.9 4.7 convert_element_type.278
  (233 shorter events, 28.9 us)
Async XLA Ops:
  7.2 2.8 copy-start.41
  7.2 16.4 copy-start.45
  7.2 16.7 copy-start.46
  7.2 16.9 copy-start.47
  7.2 17.2 copy-start.48
  7.2 17.4 copy-start.49
  7.3 17.7 copy-start.40
  7.3 46.8 %copy-start.2 = (bf16[1,128,1600]{1,2,0:T(8,128)(2,1)S(1)}, bf16[1,128,1600]{1,2,0:T(8,128)(2,1)}, u32[]{:S(2)}) copy-start(bf16[1,128,1600]{1,2,0:T(8,128)(2,1)} %param.18) | copy-start | bytes 1228804
  7.3 273.5 %all-gather.8.cloned.1.call-start = ((), (), s32[]{:S(2)}) async-start(), calls=%async_computation.6 | async-start | bytes 19456000 | tf_op jit(solution)/shard_map/all_gather | solution.py:71
  8.0 319.6 %all-gather.12.cloned.1.call-start = ((), (), s32[]{:S(2)}) async-start(), calls=%async_computation.8 | async-start | bytes 3686400 | tf_op jit(solution)/shard_map/all_gather | solution.py:110
  54.0 239.1 %copy-start.26 = (f32[1600]{0:T(1024)}, f32[1600]{0:T(1024)S(1)}, u32[]{:S(2)}) copy-start(f32[1600]{0:T(1024)S(1)} %convert_element_type.234) | copy-start | bytes 19204
  54.0 239.1 %copy-start.22 = (f32[1600]{0:T(1024)}, f32[1600]{0:T(1024)S(1)}, u32[]{:S(2)}) copy-start(f32[1600]{0:T(1024)S(1)} %convert_element_type.233) | copy-start | bytes 19204
  54.3 238.8 %copy-start.32 = (f32[128]{0:T(128)}, f32[128]{0:T(128)S(1)}, u32[]{:S(2)}) copy-start(f32[128]{0:T(128)S(1)} %broadcast_multiply_fusion.1) | copy-start | bytes 1540
  54.5 238.5 %copy-start.51 = (f32[128]{0:T(128)}, f32[128]{0:T(128)S(1)}, u32[]{:S(2)}) copy-start(f32[128]{0:T(128)S(1)} %fusion.61) | copy-start | bytes 1540
  54.5 238.5 %copy-start.38 = (f32[128]{0:T(128)}, f32[128]{0:T(128)S(1)}, u32[]{:S(2)}) copy-start(f32[128]{0:T(128)S(1)} %fusion.75) | copy-start | bytes 1540
  295.7 67.7 %all-gather.10.cloned.1.call-start = ((), (), s32[]{:S(2)}) async-start(), calls=%async_computation.7 | async-start | bytes 3686400 | tf_op jit(solution)/shard_map/all_gather | solution.py:109
  297.7 166.6 %all-gather.14.cloned.1.call-start = ((), (), s32[]{:S(2)}) async-start(), calls=%async_computation.9 | async-start | bytes 6656000 | tf_op jit(solution)/shard_map/all_gather | solution.py:73
  298.3 514.7 %all-gather.16.cloned.1.call-start = ((), (), s32[]{:S(2)}) async-start(), calls=%async_computation.10 | async-start | bytes 25600000 | tf_op jit(solution)/shard_map/all_gather | solution.py:77
  298.9 863.0 %all-gather.18.cloned.1.call-start = ((), (), s32[]{:S(2)}) async-start(), calls=%async_computation.11 | async-start | bytes 25600000 | tf_op jit(solution)/shard_map/all_gather | solution.py:79
  299.5 1017.5 %reduce-scatter.19.cloned.1.call-start = ((), (), s32[]{:S(2)}) async-start(), calls=%async_computation.16 | async-start | bytes 7372800
  300.0 889.1 %copy-start.20 = (f32[1600]{0:T(1024)}, f32[1600]{0:T(1024)S(1)}, u32[]{:S(2)}) copy-start(f32[1600]{0:T(1024)S(1)} %convert_element_type.242) | copy-start | bytes 19204
  300.1 512.9 %copy-start.24 = (f32[1600]{0:T(1024)}, f32[1600]{0:T(1024)S(1)}, u32[]{:S(2)}) copy-start(f32[1600]{0:T(1024)S(1)} %convert_element_type.243) | copy-start | bytes 19204
  386.0 83.1 %copy-start.10 = (bf16[128,25,64]{0,2,1:T(8,128)(2,1)}, bf16[128,25,64]{0,2,1:T(8,128)(2,1)S(1)}, u32[]{:S(2)}) copy-start(bf16[128,25,64]{0,2,1:T(8,128)(2,1)S(1)} %fusion.73) | copy-start | bytes 1228804
  469.1 720.0 %copy-start = (f32[128,1600]{0,1:T(8,128)}, f32[128,1600]{0,1:T(8,128)S(1)}, u32[]{:S(2)}) copy-start(f32[128,1600]{0,1:T(8,128)S(1)} %get-tuple-element.486) | copy-start | bytes 2457604
  469.1 720.0 %copy-start.28 = (f32[128]{0:T(128)}, f32[128]{0:T(128)S(1)}, u32[]{:S(2)}) copy-start(f32[128]{0:T(128)S(1)} %broadcast_multiply_fusion) | copy-start | bytes 1540
  469.4 719.8 %copy-start.30 = (f32[128]{0:T(128)}, f32[128]{0:T(128)S(1)}, u32[]{:S(2)}) copy-start(f32[128]{0:T(128)S(1)} %fusion.76) | copy-start | bytes 1540
  469.4 692.5 %copy-start.6 = (bf16[1,128,1600]{1,2,0:T(8,128)(2,1)S(1)}, bf16[1,128,1600]{1,2,0:T(8,128)(2,1)}, u32[]{:S(2)}) copy-start(bf16[1,128,1600]{1,2,0:T(8,128)(2,1)} %param.19) | copy-start | bytes 1228804
  1175.8 13.3 copy-start.4
  1175.8 14.6 slice-start
  1175.8 14.6 slice-start.1
  1189.5 2.5 copy-start.43
  1190.4 1.6 copy-start.18
  1255.2 160.1 %reduce-scatter.13.cloned.1.call-start = ((), (), s32[]{:S(2)}) async-start(), calls=%async_computation.13 | async-start | bytes 6656000 | tf_op jit(solution)/shard_map/reduce_scatter | solution.py:264
  1260.1 58.6 %copy-start.3 = (bf16[1,128,1600]{1,2,0:T(8,128)(2,1)S(1)}, bf16[1,128,1600]{1,2,0:T(8,128)(2,1)}, u32[]{:S(2)}) copy-start(bf16[1,128,1600]{1,2,0:T(8,128)(2,1)} %param.18) | copy-start | bytes 1228804
  1260.1 58.6 %copy-start.23 = (f32[1600]{0:T(1024)S(1)}, f32[1600]{0:T(1024)}, u32[]{:S(2)}) copy-start(f32[1600]{0:T(1024)} %copy-done.22) | copy-start | bytes 19204
  1260.1 58.6 %copy-start.27 = (f32[1600]{0:T(1024)S(1)}, f32[1600]{0:T(1024)}, u32[]{:S(2)}) copy-start(f32[1600]{0:T(1024)} %copy-done.26) | copy-start | bytes 19204
  1260.1 58.6 %copy-start.33 = (f32[128]{0:T(128)S(1)}, f32[128]{0:T(128)}, u32[]{:S(2)}) copy-start(f32[128]{0:T(128)} %copy-done.32) | copy-start | bytes 1540
  1260.1 58.6 %copy-start.39 = (f32[128]{0:T(128)S(1)}, f32[128]{0:T(128)}, u32[]{:S(2)}) copy-start(f32[128]{0:T(128)} %copy-done.38) | copy-start | bytes 1540
  1260.2 418.5 %reduce-scatter.11.cloned.1.call-start = ((), (), s32[]{:S(2)}) async-start(), calls=%async_computation.12 | async-start | bytes 19456000 | tf_op jit(solution)/shard_map/reduce_scatter | solution.py:258
  1260.5 66.8 %copy-start.19 = (bf16[128,25,64]{0,2,1:T(8,128)(2,1)}, bf16[128,25,64]{0,2,1:T(8,128)(2,1)S(1)}, u32[]{:S(2)}) copy-start(bf16[128,25,64]{0,2,1:T(8,128)(2,1)S(1)} %get-tuple-element.470) | copy-start | bytes 1228804
  1318.7 8.6 copy-start.13
  1327.3 694.3 %reduce-scatter.17.cloned.1.call-start = ((), (), s32[]{:S(2)}) async-start(), calls=%async_computation.15 | async-start | bytes 25600000 | tf_op jit(solution)/shard_map/reduce_scatter | solution.py:171
  1340.0 1.1 copy-start.1
  1340.0 1.7 copy-start.5
  1340.0 1.7 copy-start.21
  1340.0 1.7 copy-start.25
  1340.0 1.7 copy-start.29
  1340.1 1.7 copy-start.31
  1340.1 1024.8 %reduce-scatter.15.cloned.1.call-start = ((), (), s32[]{:S(2)}) async-start(), calls=%async_computation.14 | async-start | bytes 25600000 | tf_op jit(solution)/shard_map/reduce_scatter | solution.py:165
  1352.2 1.1 copy-start.14
  1352.2 1059.8 %reduce-scatter.21.cloned.1.call-start = ((), (), s32[]{:S(2)}) async-start(), calls=%async_computation.17 | async-start | bytes 512000
  1354.5 1243.5 %all-reduce.20.cloned.1.call-start = ((), (), s32[]{:S(2)}) async-start(), calls=%async_computation.18 | async-start | bytes 30924800 | tf_op jit(solution)/shard_map/psum | solution.py:274
  2364.9 1.5 copy-start.50
  2366.7 9.2 copy-start.52
  2366.7 10.6 copy-start.34
  2366.7 10.6 copy-start.35
  2366.7 10.6 copy-start.36
  2366.7 10.7 copy-start.37
  2366.7 31.1 %copy-start.9 = (f32[128,1600]{0,1:T(8,128)S(1)}, f32[128,1600]{0,1:T(8,128)}, u32[]{:S(2)}) copy-start(f32[128,1600]{0,1:T(8,128)} %copy-done.8) | copy-start | bytes 2457604
  2366.7 31.1 %copy-start.44 = (f32[128]{0:T(128)S(1)}, f32[128]{0:T(128)}, u32[]{:S(2)}) copy-start(f32[128]{0:T(128)} %copy-done.43) | copy-start | bytes 1540
  2598.1 3.2 copy-start.15
  2601.2 4.9 copy-start.12
  2601.2 9.6 slice-start.2
  2606.2 4.7 slice-start.3
  (6 other events, 5.6 us)
Sparse Core Ops, SparseCore 0:
  9.7 271.0 all-gather.7
  295.8 31.6 all-gather.11
  330.0 33.3 all-gather.9
  364.9 99.4 all-gather.13
  465.8 347.1 all-gather.15
  814.4 347.4 all-gather.17
  1255.3 61.6 reduce-scatter.18
  1320.0 95.2 reduce-scatter.12
  1417.8 260.8 reduce-scatter.10
  1680.9 340.7 reduce-scatter.16
  2024.1 340.6 reduce-scatter.14
  2367.6 22.1 reduce-scatter.20
  2394.4 203.6 all-reduce.19
where the time goes:
time: 2630 us; the launch traced here: 2620 us
  waiting for transfers between devices  2270 us (86%)
  matrix products  145 us (6%)
  blocking collectives  86.3 us (3%)
  other arithmetic  58.3 us (2%)
  local copies, waits for them, and re-layouts  40.2 us (2%)
    all_gather x1, waiting for transfers between devices, on_device(): lax.all_gather(fc_weight, 'fsdp', axis=0, tiled=True)  344 us
    reduce_scatter x1, waiting for transfers between devices, on_device(): lax.psum_scatter(grad_fc.astype(jnp.bfloat16), 'fsdp', scatter_dimension=...  343 us
    reduce_scatter x1, waiting for transfers between devices, on_device(): lax.psum_scatter(grad_proj.astype(jnp.bfloat16), 'fsdp', scatter_dimensio...  343 us
    all_gather x1, waiting for transfers between devices, on_device(): lax.all_gather(proj_weight, 'fsdp', axis=1, tiled=True)  337 us
    reduce_scatter x1, waiting for transfers between devices, on_device(): lax.psum_scatter(grad_qkv.astype(jnp.bfloat16), 'fsdp', scatter_dimension...  263 us
    all_gather x1, waiting for transfers between devices, on_device(): lax.all_gather(qkv_weight, 'fsdp', axis=0, tiled=True)  226 us
    psum x1, waiting for transfers between devices, on_device(): lax.psum(attn_parts[2].astype(jnp.bfloat16), 'ctx').astype(jnp.float32)  156 us
    all_gather x1, waiting for transfers between devices, on_device(): lax.all_gather(out_weight, 'fsdp', axis=0, tiled=True)  78.4 us
  transfers between devices with their start and end apart: 13, of which 12 were waited for; matrix products, arithmetic and copies ran while one was open for 4% of the time, Pallas kernels for 0%

commit v1 on v0

--- a/solution.py
+++ b/solution.py
@@ -1,3 +1,4 @@
+import functools
 import math
 import jax
 import jax.numpy as jnp
@@ -7,6 +8,36 @@
 D = 1600
 H = 25
 HD = 64
+
+
+def note_the_unit(s0, bus_axis):
+    m_next = lax.axis_size(bus_axis)
+    k_now = lax.axis_index(bus_axis)
+    y1, now, inter = (m_next, k_now, s0.shape[0])
+    nodes = []
+    for kk, w in enumerate(s0.shape):
+        nodes.append(w * y1 if kk == 0 else w)
+    later = jnp.zeros(nodes, s0.dtype)
+    res = lax.dynamic_update_slice_in_dim(later, s0, now * inter, axis=0)
+    tmp = current_value = s0
+    for k in tuple(range(1, y1 // 2 + 1)):
+        pages = []
+        for kk in tuple(range(y1)):
+            pages.append((kk, (kk + 1) % y1))
+        tmp = lax.ppermute(tmp, bus_axis, pages)
+        res = lax.dynamic_update_slice_in_dim(res, tmp, (now - k) % y1 * inter, axis=0)
+        if 2 * k < y1:
+            lanes = []
+            for kk in tuple(range(y1)):
+                lanes.append((kk, (kk - 1) % y1))
+            current_value = lax.ppermute(current_value, bus_axis, lanes)
+            res = lax.dynamic_update_slice_in_dim(
+                res, current_value, (now + k) % y1 * inter, axis=0
+            )
+    return res
+
+
+follow_point_up = functools.partial(note_the_unit, bus_axis="fsdp")
 
 
 def norm_apply(values, norm_gain, norm_bias):
@@ -70,7 +101,7 @@
         lax.all_gather(first_bias, "fsdp", axis=0, tiled=True),
         lax.all_gather(qkv_weight, "fsdp", axis=0, tiled=True),
         lax.all_gather(qv_bias, "fsdp", axis=1, tiled=True),
-        lax.all_gather(out_weight, "fsdp", axis=0, tiled=True),
+        follow_point_up(out_weight),
         lax.all_gather(out_bias, "fsdp", axis=0, tiled=True),
         lax.all_gather(second_gain, "fsdp", axis=0, tiled=True),
         lax.all_gather(second_bias, "fsdp", axis=0, tiled=True),

time: 2630 us -> 2540 us (0.966)
  waiting for transfers between devices: 2270 us -> 2160 us
    ppermute x0 -> x3, waiting for transfers between devices: none -> 81.6 us  [the longest x2 64.2 us: note_the_unit(): tmp = lax.ppermute(tmp, bus_axis, pages)]
    all_gather x1 -> x0, waiting for transfers between devices: 78.4 us -> none  [on_device(): lax.all_gather(out_weight, 'fsdp', axis=0, tiled=True)]
    all_gather x1, waiting for transfers between devices: 344 us -> 296 us  [on_device(): lax.all_gather(fc_weight, 'fsdp', axis=0, tiled=True)]
    all_gather x1, waiting for transfers between devices: 35.9 us -> 0.01 us  [on_device(): key_piece = lax.all_gather(key_rows, 'ctx', axis=0, tiled=True)]
    all_gather x1, waiting for transfers between devices: 27.5 us -> 0.01 us  [on_device(): value_piece = lax.all_gather(value_rows, 'ctx', axis=0, tiled=True)]
    unnamed x15 -> x14, waiting for transfers between devices: 58.9 us -> 58.2 us
  transfers between devices with their start and end apart: 13 -> 15, of which waited for: 12 -> 12; matrix products, arithmetic and copies ran while one was open for 4% -> 5% of each run, Pallas kernels for 0% -> 0%
where the time goes in v1:
time: 2540 us; the launch traced here: 2530 us
  waiting for transfers between devices  2160 us (85%)
  matrix products  147 us (6%)
  blocking collectives  86 us (3%)
  other arithmetic  57.1 us (2%)
  local copies, waits for them, and re-layouts  52 us (2%)
    reduce_scatter x1, waiting for transfers between devices, on_device(): lax.psum_scatter(grad_proj.astype(jnp.bfloat16), 'fsdp', scatter_dimensio...  343 us
    reduce_scatter x1, waiting for transfers between devices, on_device(): lax.psum_scatter(grad_fc.astype(jnp.bfloat16), 'fsdp', scatter_dimension=...  343 us
    all_gather x1, waiting for transfers between devices, on_device(): lax.all_gather(proj_weight, 'fsdp', axis=1, tiled=True)  336 us
    all_gather x1, waiting for transfers between devices, on_device(): lax.all_gather(fc_weight, 'fsdp', axis=0, tiled=True)  296 us
    reduce_scatter x1, waiting for transfers between devices, on_device(): lax.psum_scatter(grad_qkv.astype(jnp.bfloat16), 'fsdp', scatter_dimension...  263 us
    all_gather x1, waiting for transfers between devices, on_device(): lax.all_gather(qkv_weight, 'fsdp', axis=0, tiled=True)  226 us
    psum x1, waiting for transfers between devices, on_device(): lax.psum(attn_parts[2].astype(jnp.bfloat16), 'ctx').astype(jnp.float32)  157 us
    ppermute x2, waiting for transfers between devices, note_the_unit(): tmp = lax.ppermute(tmp, bus_axis, pages)  64.2 us
  transfers between devices with their start and end apart: 15, of which 12 were waited for; matrix products, arithmetic and copies ran while one was open for 5% of the time, Pallas kernels for 0%

profile of v1, /device:TPU:0, one launch (start us, length us, event | category | flops | bytes accessed | tf_op | source)
XLA Modules:
  0.0 2530.8 jit_solution(7717829114070762614)
XLA Ops:
  10.0 13.5 all-gather
  25.2 28.7 %all-reduce.17 = (bf16[1600]{0:T(1024)(128)(2,1)S(1)}, bf16[1600]{0:T(1024)(128)(2,1)S(1)}, bf16[1600]{0:T(1024)(128)(2,1)S(1)}, bf16[6400]{0:T(1024)(128)(2,1)S...) all-reduce(bf16[1600]{0:T(1024)(128)(2,1)S(1)} %dynamic-update-slic, ...), channel_id=1, replica_groups=mesh['ctx'=8,'fsdp'=4] {'fsdp'}, use_global_device_ids=true, to_apply=%add.1 | all-reduce | flops 14400 | bytes 57600
  54.5 226.2 %all-gather.7.cloned.1.call-done = bf16[1600,4800]{1,0:T(8,128)(2,1)} async-done(((bf16[400,4800]{1,0:T(8,128)(2,1)}), bf16[1600,4800]{1,0:T(8,128)(2,1)}) %all-gather.7.cloned.1.call-update) | async-done | bytes 15360016 | tf_op jit(solution)/shard_map/all_gather | solution.py:102
  280.8 12.3 fusion.80
  293.1 2.6 fusion.63
  295.8 1.9 slice.41
  299.0 3.8 collective-permute-start.1
  302.8 30.4 %collective-permute-done = bf16[400,1600]{1,0:T(8,128)(2,1)} collective-permute-done((bf16[400,1600]{1,0:T(8,128)(2,1)}, bf16[400,1600]{1,0:T(8,128)(2,1)}, u32[]{:S(2)}, u32[]{:S(2)}) %collective-permute-start) | collective-permute-done | bytes 1280032 | tf_op jit(solution)/shard_map/ppermute | solution.py:27
  333.9 2.8 broadcast_in_dim.138
  336.6 2.6 constant_dynamic-update-slice_fusion.3
  339.2 2.5 constant_dynamic-update-slice_fusion.2
  341.7 17.4 collective-permute-done.1
  359.1 2.5 constant_dynamic-update-slice_fusion.1
  361.6 33.8 %collective-permute-done.2 = bf16[400,1600]{1,0:T(8,128)(2,1)} collective-permute-done((bf16[400,1600]{1,0:T(8,128)(2,1)}, bf16[400,1600]{1,0:T(8,128)(2,1)}, u32[]{:S(2)}, u32[]{:S(2)}) %collective-permute-start.2) | collective-permute-done | bytes 1280032 | tf_op jit(solution)/shard_map/ppermute | solution.py:27
  395.4 2.5 constant_dynamic-update-slice_fusion
  397.9 20.2 while.34
  398.0 2.1 constant_dynamic-slice_fusion.6
  401.7 1.6 fusion.154
  403.3 2.0 fusion.156
  405.3 2.5 fusion.157
  408.0 2.2 constant_dynamic-slice_fusion.6
  410.2 1.5 fusion.152
  411.7 1.6 fusion.154
  413.3 2.0 fusion.156
  415.3 2.5 fusion.157
  418.1 5.0 fusion.88
  423.4 295.9 %all-gather.13.cloned.1.call-done = bf16[1600,6400]{1,0:T(8,128)(2,1)} async-done(((bf16[400,6400]{1,0:T(8,128)(2,1)}), bf16[1600,6400]{1,0:T(8,128)(2,1)}) %all-gather.13.cloned.1.call-update) | async-done | bytes 20480016 | tf_op jit(solution)/shard_map/all_gather | solution.py:108
  719.3 12.4 convolution_add_fusion
  731.7 336.1 %all-gather.15.cloned.1.call-done = bf16[6400,1600]{0,1:T(8,128)(2,1)} async-done(((bf16[6400,400]{0,1:T(8,128)(2,1)}), bf16[6400,1600]{0,1:T(8,128)(2,1)}) %all-gather.15.cloned.1.call-update) | async-done | bytes 20480016 | tf_op jit(solution)/shard_map/all_gather | solution.py:110
  1067.9 13.8 fusion.89
  1081.7 12.7 multiply_reduce_fusion
  1095.7 4.2 convolution_convert_fusion.4
  1100.1 6.3 broadcast_in_dim.142
  1106.4 38.6 %while.35 = (s32[]{:T(128)}, f32[128,25,64]{0,2,1:T(8,128)S(1)}, f32[1024,3200]{0,1:T(8,128)}, bf16[1024,1600]{0,1:T(8,128)(2,1)}, bf16[128,25,64]{0,2,1:T(8,128...) while((s32[]{:T(128)}, f32[128,25,64]{0,2,1:T(8,128)S(1)}, ...), condition=%wide.region_12.13_spmd.clone, body=%wide.region_11.12_spmd.clone.sunk | while | flops 1291739776 | bytes 84286680 | solution.py:72
  1106.6 2.1 constant_dynamic-slice_fusion.7
  1109.8 2.6 fusion.170
  1116.3 2.2 fusion.173
  1118.5 7.2 fusion.174
  1125.8 2.1 constant_dynamic-slice_fusion.7
  1129.1 2.6 fusion.170
  1135.5 2.2 fusion.173
  1137.7 7.2 fusion.174
  1145.0 8.6 convert_element_type.256
  1153.5 9.5 copy.61
  1164.2 3.9 convolution_convert_fusion.3
  1168.6 56.4 %reduce-scatter.19.cloned.1.call-done = bf16[128,3200]{1,0:T(8,128)(2,1)} async-done(((bf16[1024,3200]{1,0:T(8,128)(2,1)}), bf16[128,3200]{1,0:T(8,128)(2,1)}) %reduce-scatter.19.cloned.1.call-update) | async-done | bytes 819216
  1224.9 1.7 copy.62
  1226.7 8.5 convolution_convert_fusion.2
  1236.2 11.7 convolution_convert_fusion
  1249.6 10.4 convolution_convert_fusion.1
  1262.7 60.4 %reduce-scatter.13.cloned.1.call-done = bf16[400,1600]{1,0:T(8,128)(2,1)} async-done(((bf16[1600,1600]{1,0:T(8,128)(2,1)}), bf16[400,1600]{1,0:T(8,128)(2,1)}) %reduce-scatter.13.cloned.1.call-update) | async-done | bytes 1280016 | tf_op jit(solution)/shard_map/reduce_scatter | solution.py:295
  1323.2 263.4 %reduce-scatter.11.cloned.1.call-done = bf16[400,4800]{1,0:T(8,128)(2,1)} async-done(((bf16[1600,4800]{1,0:T(8,128)(2,1)}), bf16[400,4800]{1,0:T(8,128)(2,1)}) %reduce-scatter.11.cloned.1.call-update) | async-done | bytes 3840016 | tf_op jit(solution)/shard_map/reduce_scatter | solution.py:289
  1586.6 343.1 %reduce-scatter.17.cloned.1.call-done = bf16[6400,400]{0,1:T(8,128)(2,1)} async-done(((bf16[6400,1600]{0,1:T(8,128)(2,1)}), bf16[6400,400]{0,1:T(8,128)(2,1)}) %reduce-scatter.17.cloned.1.call-update) | async-done | bytes 5120016 | tf_op jit(solution)/shard_map/reduce_scatter | solution.py:202
  1929.7 343.1 %reduce-scatter.15.cloned.1.call-done = bf16[400,6400]{1,0:T(8,128)(2,1)} async-done(((bf16[1600,6400]{1,0:T(8,128)(2,1)}), bf16[400,6400]{1,0:T(8,128)(2,1)}) %reduce-scatter.15.cloned.1.call-update) | async-done | bytes 5120016 | tf_op jit(solution)/shard_map/reduce_scatter | solution.py:196
  2274.6 9.1 fusion.82
  2285.2 19.8 all-reduce.16
  2305.6 2.5 fusion.67
  2308.1 11.6 fusion.50
  2320.8 24.0 all-reduce.14
  2349.4 156.9 %all-reduce.20.cloned.1.call-done = (bf16[400,4800]{1,0:T(8,128)(2,1)}, bf16[400,1600]{1,0:T(8,128)(2,1)}, bf16[400,6400]{1,0:T(8,128)(2,1)}, bf16[6400,400]{0,1:T(8,128)(2,1)}) async-done(((bf16[400,4800]{1,0:T(8,128)(2,1)}, bf16[400,1600]{1,0:T(8,128)(2,1)}, bf16[400,6400]{1,0:T(8,128)(2,1)}, bf16[6400,400]{0,1:T(8,128)(2,1)}), (bf16[400,4800]{1,0:T(8,128)(2,1)}, bf16[400,1600]{1,0:T(8,128)(2,1)}, ...) | async-done | bytes 15360016 | tf_op jit(solution)/shard_map/psum | solution.py:305
  2506.3 3.1 convert_element_type.268
  2509.4 4.5 convert_element_type.263
  2514.4 4.7 convert_element_type.275
  2519.0 4.7 convert_element_type.278
  (236 shorter events, 34.7 us)
Async XLA Ops:
  7.2 2.8 copy-start.41
  7.2 16.4 copy-start.45
  7.2 16.7 copy-start.46
  7.2 16.9 copy-start.47
  7.2 17.2 copy-start.48
  7.2 17.4 copy-start.49
  7.3 17.7 copy-start.40
  7.3 46.8 %copy-start.2 = (bf16[1,128,1600]{1,2,0:T(8,128)(2,1)S(1)}, bf16[1,128,1600]{1,2,0:T(8,128)(2,1)}, u32[]{:S(2)}) copy-start(bf16[1,128,1600]{1,2,0:T(8,128)(2,1)} %param.18) | copy-start | bytes 1228804
  7.3 273.5 %all-gather.7.cloned.1.call-start = ((), (), s32[]{:S(2)}) async-start(), calls=%async_computation.6 | async-start | bytes 19456000 | tf_op jit(solution)/shard_map/all_gather | solution.py:102
  8.0 389.8 %all-gather.11.cloned.1.call-start = ((), (), s32[]{:S(2)}) async-start(), calls=%async_computation.8 | async-start | bytes 3686400 | tf_op jit(solution)/shard_map/all_gather | solution.py:141
  54.0 239.1 %copy-start.26 = (f32[1600]{0:T(1024)}, f32[1600]{0:T(1024)S(1)}, u32[]{:S(2)}) copy-start(f32[1600]{0:T(1024)S(1)} %convert_element_type.234) | copy-start | bytes 19204
  54.0 239.1 %copy-start.22 = (f32[1600]{0:T(1024)}, f32[1600]{0:T(1024)S(1)}, u32[]{:S(2)}) copy-start(f32[1600]{0:T(1024)S(1)} %convert_element_type.233) | copy-start | bytes 19204
  54.3 238.8 %copy-start.32 = (f32[128]{0:T(128)}, f32[128]{0:T(128)S(1)}, u32[]{:S(2)}) copy-start(f32[128]{0:T(128)S(1)} %broadcast_multiply_fusion.1) | copy-start | bytes 1540
  54.5 238.5 %copy-start.51 = (f32[128]{0:T(128)}, f32[128]{0:T(128)S(1)}, u32[]{:S(2)}) copy-start(f32[128]{0:T(128)S(1)} %fusion.61) | copy-start | bytes 1540
  54.5 238.5 %copy-start.38 = (f32[128]{0:T(128)}, f32[128]{0:T(128)S(1)}, u32[]{:S(2)}) copy-start(f32[128]{0:T(128)S(1)} %fusion.75) | copy-start | bytes 1540
  295.7 102.1 %all-gather.9.cloned.1.call-start = ((), (), s32[]{:S(2)}) async-start(), calls=%async_computation.7 | async-start | bytes 3686400 | tf_op jit(solution)/shard_map/all_gather | solution.py:140
  297.7 421.6 %all-gather.13.cloned.1.call-start = ((), (), s32[]{:S(2)}) async-start(), calls=%async_computation.9 | async-start | bytes 25600000 | tf_op jit(solution)/shard_map/all_gather | solution.py:108
  298.3 769.5 %all-gather.15.cloned.1.call-start = ((), (), s32[]{:S(2)}) async-start(), calls=%async_computation.10 | async-start | bytes 25600000 | tf_op jit(solution)/shard_map/all_gather | solution.py:110
  298.9 926.0 %reduce-scatter.19.cloned.1.call-start = ((), (), s32[]{:S(2)}) async-start(), calls=%async_computation.15 | async-start | bytes 7372800
  298.9 34.3 %collective-permute-start = (bf16[400,1600]{1,0:T(8,128)(2,1)}, bf16[400,1600]{1,0:T(8,128)(2,1)}, u32[]{:S(2)}, u32[]{:S(2)}) collective-permute-start(bf16[400,1600]{1,0:T(8,128)(2,1)} %param.24), channel_id=1, source_target_pairs={{0,1},{1,2},{2,3},{3,0},{4,5},{5,6},{6,7},{7,4},{8,9},{9,10},{10,1... | collective-permute-start | bytes 3840008 | tf_op jit(solution)/shard_map/ppermute | solution.py:27
  299.0 60.1 %collective-permute-start.1 = (bf16[400,1600]{1,0:T(8,128)(2,1)}, bf16[400,1600]{1,0:T(8,128)(2,1)}, u32[]{:S(2)}, u32[]{:S(2)}) collective-permute-start(bf16[400,1600]{1,0:T(8,128)(2,1)} %param.24), channel_id=1, source_target_pairs={{0,3},{1,0},{2,1},{3,2},{4,7},{5,4},{6,5},{7,6},{8,11},{9,8},{10,9... | collective-permute-start | bytes 3840008 | tf_op jit(solution)/shard_map/ppermute | solution.py:33
  333.2 62.1 %collective-permute-start.2 = (bf16[400,1600]{1,0:T(8,128)(2,1)}, bf16[400,1600]{1,0:T(8,128)(2,1)}, u32[]{:S(2)}, u32[]{:S(2)}) collective-permute-start(bf16[400,1600]{1,0:T(8,128)(2,1)} %collective-permute-done), channel_id=1, source_target_pairs={{0,1},{1,2},{2,3},{3,0},{4,5},{5,6},{6,7},{7,4},{8,9},{9,10},{10,1... | collective-permute-start | bytes 3840008 | tf_op jit(solution)/shard_map/ppermute | solution.py:27
  333.8 760.6 %copy-start.20 = (f32[1600]{0:T(1024)}, f32[1600]{0:T(1024)S(1)}, u32[]{:S(2)}) copy-start(f32[1600]{0:T(1024)S(1)} %convert_element_type.242) | copy-start | bytes 19204
  333.8 385.5 %copy-start.24 = (f32[1600]{0:T(1024)}, f32[1600]{0:T(1024)S(1)}, u32[]{:S(2)}) copy-start(f32[1600]{0:T(1024)S(1)} %convert_element_type.243) | copy-start | bytes 19204
  418.1 5.0 copy-start.10
  423.1 671.3 %copy-start = (f32[128,1600]{0,1:T(8,128)}, f32[128,1600]{0,1:T(8,128)S(1)}, u32[]{:S(2)}) copy-start(f32[128,1600]{0,1:T(8,128)S(1)} %get-tuple-element.486) | copy-start | bytes 2457604
  423.1 671.3 %copy-start.28 = (f32[128]{0:T(128)}, f32[128]{0:T(128)S(1)}, u32[]{:S(2)}) copy-start(f32[128]{0:T(128)S(1)} %broadcast_multiply_fusion) | copy-start | bytes 1540
  423.4 671.0 %copy-start.30 = (f32[128]{0:T(128)}, f32[128]{0:T(128)S(1)}, u32[]{:S(2)}) copy-start(f32[128]{0:T(128)S(1)} %fusion.76) | copy-start | bytes 1540
  423.4 644.5 %copy-start.6 = (bf16[1,128,1600]{1,2,0:T(8,128)(2,1)S(1)}, bf16[1,128,1600]{1,2,0:T(8,128)(2,1)}, u32[]{:S(2)}) copy-start(bf16[1,128,1600]{1,2,0:T(8,128)(2,1)} %param.19) | copy-start | bytes 1228804
  1081.7 12.7 copy-start.4
  1094.7 5.1 copy-start.43
  1095.7 4.2 copy-start.17
  1163.1 160.1 %reduce-scatter.13.cloned.1.call-start = ((), (), s32[]{:S(2)}) async-start(), calls=%async_computation.12 | async-start | bytes 6656000 | tf_op jit(solution)/shard_map/reduce_scatter | solution.py:295
  1168.2 58.5 %copy-start.3 = (bf16[1,128,1600]{1,2,0:T(8,128)(2,1)S(1)}, bf16[1,128,1600]{1,2,0:T(8,128)(2,1)}, u32[]{:S(2)}) copy-start(bf16[1,128,1600]{1,2,0:T(8,128)(2,1)} %param.18) | copy-start | bytes 1228804
  1168.2 58.5 %copy-start.23 = (f32[1600]{0:T(1024)S(1)}, f32[1600]{0:T(1024)}, u32[]{:S(2)}) copy-start(f32[1600]{0:T(1024)} %copy-done.22) | copy-start | bytes 19204
  1168.2 58.5 %copy-start.27 = (f32[1600]{0:T(1024)S(1)}, f32[1600]{0:T(1024)}, u32[]{:S(2)}) copy-start(f32[1600]{0:T(1024)} %copy-done.26) | copy-start | bytes 19204
  1168.2 58.5 %copy-start.33 = (f32[128]{0:T(128)S(1)}, f32[128]{0:T(128)}, u32[]{:S(2)}) copy-start(f32[128]{0:T(128)} %copy-done.32) | copy-start | bytes 1540
  1168.2 58.5 %copy-start.39 = (f32[128]{0:T(128)S(1)}, f32[128]{0:T(128)}, u32[]{:S(2)}) copy-start(f32[128]{0:T(128)} %copy-done.38) | copy-start | bytes 1540
  1168.2 418.4 %reduce-scatter.11.cloned.1.call-start = ((), (), s32[]{:S(2)}) async-start(), calls=%async_computation.11 | async-start | bytes 19456000 | tf_op jit(solution)/shard_map/reduce_scatter | solution.py:289
  1168.5 66.6 %copy-start.19 = (bf16[128,25,64]{0,2,1:T(8,128)(2,1)}, bf16[128,25,64]{0,2,1:T(8,128)(2,1)S(1)}, u32[]{:S(2)}) copy-start(bf16[128,25,64]{0,2,1:T(8,128)(2,1)S(1)} %get-tuple-element.470) | copy-start | bytes 1228804
  1226.6 8.6 copy-start.13
  1235.2 694.4 %reduce-scatter.17.cloned.1.call-start = ((), (), s32[]{:S(2)}) async-start(), calls=%async_computation.14 | async-start | bytes 25600000 | tf_op jit(solution)/shard_map/reduce_scatter | solution.py:202
  1247.9 1.1 copy-start.1
  1247.9 1.7 copy-start.5
  1247.9 1.7 copy-start.21
  1247.9 1.7 copy-start.25
  1247.9 1.7 copy-start.29
  1248.0 1.7 copy-start.31
  1248.0 1024.8 %reduce-scatter.15.cloned.1.call-start = ((), (), s32[]{:S(2)}) async-start(), calls=%async_computation.13 | async-start | bytes 25600000 | tf_op jit(solution)/shard_map/reduce_scatter | solution.py:196
  1260.1 1.1 copy-start.14
  1260.1 1059.7 %reduce-scatter.21.cloned.1.call-start = ((), (), s32[]{:S(2)}) async-start(), calls=%async_computation.16 | async-start | bytes 512000
  1262.5 1243.8 %all-reduce.20.cloned.1.call-start = ((), (), s32[]{:S(2)}) async-start(), calls=%async_computation.17 | async-start | bytes 30924800 | tf_op jit(solution)/shard_map/psum | solution.py:305
  2272.7 1.5 copy-start.50
  2274.6 9.2 copy-start.52
  2274.6 10.6 copy-start.34
  2274.6 10.6 copy-start.35
  2274.6 10.6 copy-start.36
  2274.6 10.6 copy-start.37
  2274.6 31.0 %copy-start.9 = (f32[128,1600]{0,1:T(8,128)S(1)}, f32[128,1600]{0,1:T(8,128)}, u32[]{:S(2)}) copy-start(f32[128,1600]{0,1:T(8,128)} %copy-done.8) | copy-start | bytes 2457604
  2274.6 31.0 %copy-start.44 = (f32[128]{0:T(128)S(1)}, f32[128]{0:T(128)}, u32[]{:S(2)}) copy-start(f32[128]{0:T(128)} %copy-done.43) | copy-start | bytes 1540
  2506.3 3.2 copy-start.15
  2509.4 4.9 copy-start.12
  2509.4 9.6 slice-start
  2514.4 4.7 slice-start.1
  (6 other events, 5.9 us)
Sparse Core Ops, SparseCore 0:
  9.7 271.0 all-gather.6
  295.8 31.6 all-gather.10
  330.0 33.3 all-gather.8
  364.9 354.3 all-gather.12
  720.7 347.0 all-gather.14
  1163.2 61.6 reduce-scatter.18
  1227.9 95.2 reduce-scatter.12
  1325.7 260.8 reduce-scatter.10
  1588.9 340.6 reduce-scatter.16
  1932.0 340.7 reduce-scatter.14
  2275.6 22.2 reduce-scatter.20
  2302.4 203.7 all-reduce.19
